TPU v7x, 512 devices: a whole 4x8x8 slice. The times are simulated.
512 devices in a mesh: dp: 8 (over x, y_hi), expert: 64 (over y_lo, z, core).
Axes of the slice: x: 4, y: 8 (y_hi: 2, y_lo: 4; y = y_hi * 4 + y_lo), z: 8, core: 2. Of those that a mesh axis runs over, the one named last changes fastest.
Arguments:
- tokens: bfloat16 [65536, 3584], P(('dp', 'expert')), may hold values from -6 to 6
- out_grad: bfloat16 [65536, 3584], P(('dp', 'expert')), may hold values from -1.1953125 to 1.1953125
- gate_weight: bfloat16 [3584, 32768], P('dp', 'expert'), may hold values from -0.09375 to 0.09375
- up_weight: bfloat16 [3584, 32768], P('dp', 'expert'), may hold values from -0.09375 to 0.09375
- route_ids: int32 [65536, 8], P(('dp', 'expert')), may hold values from 0 to 255, all different within a row; in each aligned block of 128 rows (0 to 127, 128 to 255, ...) at most 6 rows name the same one
- route_weights: float32 [65536, 8], P(('dp', 'expert')), may hold values from 0.02 to 0.5
Outputs:
- grad_down: bfloat16 [32768, 3584], P(('expert', 'dp'))
Inputs may be any that keep to these rules, and one draw needn't show every extreme that they name: `route_ids`: each row names 8 different experts. At most 6 of the rows of one device name any one expert, a bound that some block reaches.
All inputs are finite; a program needn't handle non-finite values.
Results may differ from a plain program's by a relative error of at most 0.015.
Values may be sent and summed in bfloat16 or wider, within the bound.
A program may use at most 128 MiB of HBM per device.

v0:
```python
import jax
import jax.numpy as jnp
from jax import lax
from jax.sharding import PartitionSpec as P

N_ROUTED = 256
LOG_SPLIT = 2


def pack_rows(tokens, out_grad, route_ids, route_weights, experts, row_cap):
    expert_ids = jnp.arange(experts, dtype=jnp.int32)
    matches = route_ids[:, :, None] == expert_ids[None, None, :]
    chosen = jnp.any(matches, axis=1)
    scales = jnp.sum(jnp.where(matches, route_weights[:, :, None], 0.0), axis=1)
    order_rank = jnp.cumsum(chosen.astype(jnp.int32), axis=0) - 1
    slot_ids = jnp.arange(row_cap, dtype=jnp.int32)
    pick_table = chosen.T[:, None, :] & (order_rank.T[:, None, :] == slot_ids[None, :, None])
    pick_flat = pick_table.reshape(experts * row_cap, tokens.shape[0])
    pick_values = pick_flat.astype(jnp.bfloat16)
    sent_rows = jnp.dot(pick_values, tokens, preferred_element_type=jnp.float32).astype(
        jnp.bfloat16
    )
    picked_grads = jnp.dot(pick_values, out_grad, preferred_element_type=jnp.float32)
    slot_scales = jnp.sum(jnp.where(pick_table, scales.T[:, None, :], 0.0), axis=2).reshape(
        experts * row_cap, 1
    )
    scaled = (picked_grads * slot_scales).astype(jnp.bfloat16)
    counts = jnp.sum(chosen.astype(jnp.int32), axis=0)
    return (jnp.stack([sent_rows, scaled]), counts)


def per_device(tokens, out_grad, gate_weight, up_weight, route_ids, route_weights):
    split_count = 2**LOG_SPLIT
    experts = lax.axis_size("expert") // split_count
    feature_count = tokens.shape[1]
    row_cap = max(2, tokens.shape[0] * route_ids.shape[1] * 3 // (2 * N_ROUTED))
    paired, counts = pack_rows(tokens, out_grad, route_ids, route_weights, experts, row_cap)
    spread = jnp.broadcast_to(
        paired.reshape(2, experts, 1, row_cap, feature_count),
        (2, experts, split_count, row_cap, feature_count),
    )
    spread = spread.reshape(2, experts * split_count * row_cap, feature_count)
    received = lax.all_to_all(spread, "expert", split_axis=1, concat_axis=1, tiled=True)
    rows_x = received[0]
    rows_dy = received[1]
    columns = rows_x
    gate_pre = jnp.dot(
        columns,
        lax.all_gather(gate_weight, "dp", axis=0, tiled=True),
        preferred_element_type=jnp.float32,
    )
    up_pre = jnp.dot(
        columns,
        lax.all_gather(up_weight, "dp", axis=0, tiled=True),
        preferred_element_type=jnp.float32,
    )
    hidden = (jax.nn.silu(gate_pre) * up_pre).astype(jnp.bfloat16)
    columns = hidden
    return lax.psum_scatter(
        lax.dot_general(
            columns, rows_dy, (((0,), (0,)), ((), ())), preferred_element_type=jnp.float32
        ).astype(jnp.bfloat16),
        "dp",
        scatter_dimension=0,
        tiled=True,
    )


def solution(mesh):
    return jax.shard_map(
        per_device,
        mesh=mesh,
        in_specs=(
            P(("dp", "expert"), None),
            P(("dp", "expert"), None),
            P("dp", "expert"),
            P("dp", "expert"),
            P(("dp", "expert"), None),
            P(("dp", "expert"), None),
        ),
        out_specs=P(("expert", "dp"), None),
        check_vma=False,
    )
```

profile of v0, /device:TPU:8, one launch (start us, length us, event | category | flops | bytes accessed | tf_op | source)
XLA Modules:
  0.0 417.4 jit_solution(7861766384331546865)
XLA Ops:
  6.5 0.8 fusion.18
  7.3 0.1 copy.21
  7.4 0.2 reduce_window_sum.11
  7.8 0.1 eq.43
  7.8 0.7 select_reduce_fusion.1
  8.6 0.1 select_reduce_fusion
  8.7 0.1 mul.17
  8.8 0.1 compare_and_fusion
  8.9 0.3 fusion
  9.2 0.2 stack.10
  9.4 1.5 convolution_convert_fusion.1
  11.0 0.2 stack.9
  11.2 0.4 maximum_bitcast_fusion
  11.6 1.4 copy.23
  13.1 4.0 broadcast_in_dim.43
  17.1 14.5 %all-to-all-start = ((bf16[2,384,3584]{2,0,1:T(2,128)(2,1)}), bf16[2,384,3584]{2,0,1:T(2,128)(2,1)}, u32[]{:S(2)}, u32[]{:S(2)}) async-start(bf16[2,384,3584]{2,0,1:T(2,128)(2,1)} %bitcast.27), calls=%async_computation | async-start | bytes 11010048 | tf_op jit(solution)/shard_map/all_to_all | solution.py:43
  31.6 0.7 all-gather.3.cloned.1.call-update
  32.4 0.7 all-gather.5.cloned.1.call-update
  33.1 192.5 %all-to-all-done = bf16[2,384,3584]{2,0,1:T(2,128)(2,1)} async-done(((bf16[2,384,3584]{2,0,1:T(2,128)(2,1)}), bf16[2,384,3584]{2,0,1:T(2,128)(2,1)}, u32[]{:S(2)}, u32[]{:S(2)}) %all-to-all-start) | async-done | bytes 5505056 | tf_op jit(solution)/shard_map/all_to_all | solution.py:43
  225.7 14.0 %fusion.21 = (bf16[1,384,3584]{2,0,1:T(2,128)(2,1)}, bf16[1,384,3584]{2,0,1:T(2,128)(2,1)}) fusion(bf16[2,384,3584]{2,0,1:T(2,128)(2,1)} %all-to-all-done), kind=kLoop, calls=%fused_computation.25 | loop fusion | bytes 11010048 | tf_op jit(solution)/shard_map/slice | solution.py:44
  239.7 5.2 %fusion.5 = f32[384,512]{1,0:T(8,128)S(1)} fusion(bf16[3584,512]{1,0:T(8,128)(2,1)} %all-gather.3.cloned.1.call-done, bf16[1,384,3584]{2,0,1:T(2,128)(2,1)} %get-tuple-element.5), kind=kOutput, calls=%fused_computation.8 | convolution fusion | flops 1409286144 | bytes 7208960 | tf_op jit(solution)/shard_map/dot_general | solution.py:47
  245.0 41.1 %all-gather.5.cloned.1.call-done = bf16[3584,512]{1,0:T(8,128)(2,1)} async-done(((bf16[448,512]{1,0:T(8,128)(2,1)}), bf16[3584,512]{1,0:T(8,128)(2,1)}) %all-gather.5.cloned.1.call-update) | async-done | bytes 3670032 | tf_op jit(solution)/shard_map/all_gather | solution.py:54
  286.1 10.7 %convolution_convert_fusion = bf16[512,3584]{1,0:T(8,128)(2,1)} fusion(bf16[1,384,3584]{2,0,1:T(2,128)(2,1)} %get-tuple-element.6, bf16[3584,512]{1,0:T(8,128)(2,1)} %all-gather.5.cloned.1.call-done, bf16[1,384,3584]{2,0,1:T(2,128)(2,1)} %get-tuple-element.5, f32[384,512]{1,0:T(8,128)S(1)} %fusion.5), kind=kOutput, calls=%fused_computation | convolution fusion | flops 2821586944 | bytes 13631488 | tf_op jit(solution)/shard_map/dot_general | solution.py:60
  296.8 114.0 %reduce-scatter.2.cloned.1.call-done = bf16[64,3584]{1,0:T(8,128)(2,1)} async-done(((bf16[512,3584]{1,0:T(8,128)(2,1)}), bf16[64,3584]{1,0:T(8,128)(2,1)}) %reduce-scatter.2.cloned.1.call-update) | async-done | bytes 458768 | tf_op jit(solution)/shard_map/reduce_scatter | solution.py:59
  (15 shorter events, 0.3 us)
Async XLA Ops:
  6.5 2.3 copy-start
  17.1 208.6 %all-to-all-start = ((bf16[2,384,3584]{2,0,1:T(2,128)(2,1)}), bf16[2,384,3584]{2,0,1:T(2,128)(2,1)}, u32[]{:S(2)}, u32[]{:S(2)}) async-start(bf16[2,384,3584]{2,0,1:T(2,128)(2,1)} %bitcast.27), calls=%async_computation | async-start | bytes 11010048 | tf_op jit(solution)/shard_map/all_to_all | solution.py:43
  31.6 208.1 %all-gather.3.cloned.1.call-start = ((), (), s32[]{:S(2)}) async-start(), calls=%async_computation.2 | async-start | bytes 4128768 | tf_op jit(solution)/shard_map/all_gather | solution.py:49
  32.3 253.8 %all-gather.5.cloned.1.call-start = ((), (), s32[]{:S(2)}) async-start(), calls=%async_computation.3 | async-start | bytes 4128768 | tf_op jit(solution)/shard_map/all_gather | solution.py:54
  33.1 377.7 %reduce-scatter.2.cloned.1.call-start = ((), (), s32[]{:S(2)}) async-start(), calls=%async_computation.4 | async-start | bytes 4128768 | tf_op jit(solution)/shard_map/reduce_scatter | solution.py:59
Sparse Core Ops, SparseCore 0:
  35.6 143.5 all-gather.2
  182.4 103.6 all-gather.4
  297.0 113.8 reduce-scatter.1
where the time goes:
time: 418 us; the launch traced here: 417 us
  waiting for transfers between devices  349 us (83%)
  local copies, waits for them, and re-layouts  20.3 us (5%)
  matrix products  17.8 us (4%)
  starting transfers between devices  14.6 us (3%)
  between operations  13.2 us (3%)
    all_to_all x1, waiting for transfers between devices, per_device(): lax.all_to_all(spread, 'expert', split_axis=1, concat_axis=1, tiled=True)  193 us
    reduce_scatter x1, waiting for transfers between devices, per_device(): lax.psum_scatter(lax.dot_general(columns, rows_dy, (((0,), (0,)), ((), ()...  114 us
    all_gather x1, waiting for transfers between devices, per_device(): lax.all_gather(up_weight, 'dp', axis=0, tiled=True)  41.1 us
    all_to_all x1, starting transfers between devices, per_device(): lax.all_to_all(spread, 'expert', split_axis=1, concat_axis=1, tiled=True)  14.5 us
    slice x1, local copies, waits for them, and re-layouts, per_device(): rows_x = received[0]  14 us
    dot_general x1, matrix products, per_device(): lax.dot_general(columns, rows_dy, (((0,), (0,)), ((), ())), preferred_ele...  10.7 us
  transfers between devices with their start and end apart: 4, of which 3 were waited for; matrix products, arithmetic and copies ran while one was open for 5% of the time, Pallas kernels for 0%

commit v1 on v0

--- a/solution.py
+++ b/solution.py
@@ -51,7 +51,9 @@
     )
     up_pre = jnp.dot(
         columns,
-        lax.all_gather(up_weight, "dp", axis=0, tiled=True),
+        jnp.concatenate(
+            lax.all_to_all(jnp.stack([up_weight] * lax.axis_size("dp"), axis=0), "dp", 0, 0), axis=0
+        ),
         preferred_element_type=jnp.float32,
     )
     hidden = (jax.nn.silu(gate_pre) * up_pre).astype(jnp.bfloat16)

time: 418 us -> 484 us (1.16)
  waiting for transfers between devices: 349 us -> 405 us
  starting transfers between devices: 14.6 us -> 22.2 us
    reduce_scatter x1, waiting for transfers between devices: 114 us -> 172 us  [per_device(): lax.psum_scatter(lax.dot_general(columns, rows_dy, (((0,), (0,)), ((), ()...]
    all_to_all x0 -> x1, waiting for transfers between devices: none -> 50.1 us  [per_device(): lax.all_to_all(jnp.stack([up_weight] * lax.axis_size('dp'), axis=0), 'dp'...]
    all_gather x1 -> x0, waiting for transfers between devices: 41.1 us -> none  [per_device(): lax.all_gather(up_weight, 'dp', axis=0, tiled=True)]
    all_to_all x1, waiting for transfers between devices: 193 us -> 183 us  [per_device(): lax.all_to_all(spread, 'expert', split_axis=1, concat_axis=1, tiled=True)]
    all_to_all x0 -> x1, starting transfers between devices: none -> 7.43 us  [per_device(): lax.all_to_all(jnp.stack([up_weight] * lax.axis_size('dp'), axis=0), 'dp'...]
  transfers between devices with their start and end apart: 4 -> 4, of which waited for: 3 -> 3; matrix products, arithmetic and copies ran while one was open for 5% -> 4% of each run, Pallas kernels for 0% -> 0%
where the time goes in v1:
time: 484 us
  waiting for transfers between devices  405 us (84%)
  local copies, waits for them, and re-layouts  22.5 us (5%)
  starting transfers between devices  22.2 us (5%)
  matrix products  17.8 us (4%)
  between operations  13.5 us (3%)
    all_to_all x1, waiting for transfers between devices, per_device(): lax.all_to_all(spread, 'expert', split_axis=1, concat_axis=1, tiled=True)  183 us
    reduce_scatter x1, waiting for transfers between devices, per_device(): lax.psum_scatter(lax.dot_general(columns, rows_dy, (((0,), (0,)), ((), ()...  172 us
    all_to_all x1, waiting for transfers between devices, per_device(): lax.all_to_all(jnp.stack([up_weight] * lax.axis_size('dp'), axis=0), 'dp'...  50.1 us
    all_to_all x1, starting transfers between devices, per_device(): lax.all_to_all(spread, 'expert', split_axis=1, concat_axis=1, tiled=True)  14.7 us
    slice x1, local copies, waits for them, and re-layouts, per_device(): rows_x = received[0]  14 us
    dot_general x1, matrix products, per_device(): lax.dot_general(columns, rows_dy, (((0,), (0,)), ((), ())), preferred_ele...  10.7 us
  transfers between devices with their start and end apart: 4, of which 3 were waited for; matrix products, arithmetic and copies ran while one was open for 4% of the time, Pallas kernels for 0%

profile of v1, /device:TPU:8, one launch (start us, length us, event | category | flops | bytes accessed | tf_op | source)
XLA Modules:
  0.0 483.7 jit_solution(17962650513037921193)
XLA Ops:
  6.5 0.8 fusion.18
  7.4 0.1 copy.21
  7.5 0.2 reduce_window_sum.11
  7.8 0.7 select_reduce_fusion.1
  8.6 0.1 select_reduce_fusion
  8.7 0.1 mul.17
  8.8 0.1 compare_and_fusion
  8.9 0.3 fusion
  9.2 0.2 stack.9
  9.4 1.5 convolution_convert_fusion.1
  11.0 0.2 stack.8
  11.2 0.4 maximum_bitcast_fusion
  11.6 1.4 copy.23
  13.1 4.0 broadcast_in_dim.43
  17.1 14.7 %all-to-all-start = ((bf16[2,384,3584]{2,0,1:T(2,128)(2,1)}), bf16[2,384,3584]{2,0,1:T(2,128)(2,1)}, u32[]{:S(2)}, u32[]{:S(2)}) async-start(bf16[2,384,3584]{2,0,1:T(2,128)(2,1)} %bitcast.28), calls=%async_computation | async-start | bytes 11010048 | tf_op jit(solution)/shard_map/all_to_all | solution.py:43
  31.8 0.7 all-gather.2.cloned.1.call-update
  32.5 182.9 %all-to-all-done = bf16[2,384,3584]{2,0,1:T(2,128)(2,1)} async-done(((bf16[2,384,3584]{2,0,1:T(2,128)(2,1)}), bf16[2,384,3584]{2,0,1:T(2,128)(2,1)}, u32[]{:S(2)}, u32[]{:S(2)}) %all-to-all-start) | async-done | bytes 5505056 | tf_op jit(solution)/shard_map/all_to_all | solution.py:43
  215.4 2.2 stack.11
  217.6 7.4 %all-to-all-start.1 = ((bf16[8,448,512]{2,1,0:T(8,128)(2,1)}), bf16[8,448,512]{2,1,0:T(8,128)(2,1)}, u32[]{:S(2)}, u32[]{:S(2)}) async-start(bf16[8,448,512]{2,1,0:T(8,128)(2,1)} %stack.11), calls=%async_computation.1 | async-start | bytes 7340032 | tf_op jit(solution)/shard_map/all_to_all | solution.py:55
  225.0 14.0 %fusion.21 = (bf16[1,384,3584]{2,0,1:T(2,128)(2,1)}, bf16[1,384,3584]{2,0,1:T(2,128)(2,1)}) fusion(bf16[2,384,3584]{2,0,1:T(2,128)(2,1)} %all-to-all-done), kind=kLoop, calls=%fused_computation.25 | loop fusion | bytes 11010048 | tf_op jit(solution)/shard_map/slice | solution.py:44
  239.1 5.2 %fusion.5 = f32[384,512]{1,0:T(8,128)S(1)} fusion(bf16[3584,512]{1,0:T(8,128)(2,1)} %all-gather.2.cloned.1.call-done, bf16[1,384,3584]{2,0,1:T(2,128)(2,1)} %get-tuple-element.5), kind=kOutput, calls=%fused_computation.8 | convolution fusion | flops 1409286144 | bytes 7208960 | tf_op jit(solution)/shard_map/dot_general | solution.py:47
  244.3 50.1 %all-to-all-done.1 = bf16[8,448,512]{2,1,0:T(8,128)(2,1)} async-done(((bf16[8,448,512]{2,1,0:T(8,128)(2,1)}), bf16[8,448,512]{2,1,0:T(8,128)(2,1)}, u32[]{:S(2)}, u32[]{:S(2)}) %all-to-all-start.1) | async-done | bytes 3670048 | tf_op jit(solution)/shard_map/all_to_all | solution.py:55
  294.4 10.7 %convolution_convert_fusion = bf16[512,3584]{1,0:T(8,128)(2,1)} fusion(bf16[1,384,3584]{2,0,1:T(2,128)(2,1)} %get-tuple-element.6, bf16[3584,512]{1,0:T(8,128)(2,1)} %bitcast.5, bf16[1,384,3584]{2,0,1:T(2,128)(2,1)} %get-tuple-element.5, f32[384,512]{1,0:T(8,128)S(1)} %fusion.5), kind=kOutput, calls=%fused_computation | convolution fusion | flops 2821586944 | bytes 13631488 | tf_op jit(solution)/shard_map/dot_general | solution.py:62
  305.2 171.7 %reduce-scatter.2.cloned.1.call-done = bf16[64,3584]{1,0:T(8,128)(2,1)} async-done(((bf16[512,3584]{1,0:T(8,128)(2,1)}), bf16[64,3584]{1,0:T(8,128)(2,1)}) %reduce-scatter.2.cloned.1.call-update) | async-done | bytes 458768 | tf_op jit(solution)/shard_map/reduce_scatter | solution.py:61
  (17 shorter events, 0.3 us)
Async XLA Ops:
  6.5 2.3 copy-start
  17.1 198.3 %copy-start.1 = (bf16[448,512]{1,0:T(8,128)(2,1)S(1)}, bf16[448,512]{1,0:T(8,128)(2,1)}, u32[]{:S(2)}) copy-start(bf16[448,512]{1,0:T(8,128)(2,1)} %param.9) | copy-start | bytes 1376260
  17.1 198.3 %all-to-all-start = ((bf16[2,384,3584]{2,0,1:T(2,128)(2,1)}), bf16[2,384,3584]{2,0,1:T(2,128)(2,1)}, u32[]{:S(2)}, u32[]{:S(2)}) async-start(bf16[2,384,3584]{2,0,1:T(2,128)(2,1)} %bitcast.28), calls=%async_computation | async-start | bytes 11010048 | tf_op jit(solution)/shard_map/all_to_all | solution.py:43
  31.7 207.3 %all-gather.2.cloned.1.call-start = ((), (), s32[]{:S(2)}) async-start(), calls=%async_computation.3 | async-start | bytes 4128768 | tf_op jit(solution)/shard_map/all_gather | solution.py:49
  217.6 76.9 %all-to-all-start.1 = ((bf16[8,448,512]{2,1,0:T(8,128)(2,1)}), bf16[8,448,512]{2,1,0:T(8,128)(2,1)}, u32[]{:S(2)}, u32[]{:S(2)}) async-start(bf16[8,448,512]{2,1,0:T(8,128)(2,1)} %stack.11), calls=%async_computation.1 | async-start | bytes 7340032 | tf_op jit(solution)/shard_map/all_to_all | solution.py:55
  225.0 251.9 %reduce-scatter.2.cloned.1.call-start = ((), (), s32[]{:S(2)}) async-start(), calls=%async_computation.4 | async-start | bytes 4128768 | tf_op jit(solution)/shard_map/reduce_scatter | solution.py:61
Sparse Core Ops, SparseCore 0:
  35.8 143.3 all-gather.1
  305.3 171.5 reduce-scatter.1
